TPU v7x, 32 devices: a whole 2x2x4 slice. The times are simulated.
32 devices in a mesh: grp: 2 (over y), date: 4 (over z), row: 4 (over x, core).
Axes of the slice: x: 2, y: 2, z: 4, core: 2. Of those that a mesh axis runs over, the one named last changes fastest.
Arguments:
- stack_data: float32 [16, 2, 64, 512], P(('grp', 'date'), None, 'row'), parts along dimension 0, may hold values from -40 to 40, as said below
- plan: int32 [8], replicated, may hold values from 0 to 7, each once
Outputs:
- coherence: float32 [16, 8, 2, 64, 512], P(('grp', 'date'), None, None, 'row'), parts along dimension 0
There are 2 independent parts, one for each index of `grp`. A program takes and returns all parts, laid end to end along the dimension named above; an argument that names none is the same for every part. Nothing has to cross between parts.
Inputs may be any that keep to these rules, and one draw needn't show every extreme that they name: `stack_data`: complex samples of one scene seen on every date, each date with its own phase, strength and noise.
All inputs are finite; a program needn't handle non-finite values.
Results may differ from a plain program's by a relative error of at most 0.00005.
Values sent between devices are 32-bit elements; how exact they have to be, the bound alone decides.
A program may use at most 64 MiB of HBM per device.

v0:
```python
import jax
import jax.numpy as jnp
from jax import lax
from jax.sharding import PartitionSpec as P

HALF_ROWS = 4
HALF_COLS = 16


HIGH = lax.Precision.HIGHEST
epsilon = 1e-06


def extended(array, sides, width):
    for axis, dim in sides:
        size, length = (lax.axis_size(axis), array.shape[dim])
        up = [(i, (i + 1) % size) for i in range(size - 1)]
        down = [(j, i) for i, j in up]
        last = lax.slice_in_dim(array, length - width, length, axis=dim)
        first = lax.slice_in_dim(array, 0, width, axis=dim)
        before = lax.ppermute(last, axis, up)
        after = lax.ppermute(first, axis, down)
        array = jnp.concatenate([before, array, after], axis=dim)
    return array


def body(stack_data, plan):
    rows_dev = stack_data.shape[2]
    columns = stack_data.shape[3]
    haloed = extended(stack_data, (("row", 2),), HALF_ROWS)
    row_out = lax.broadcasted_iota(jnp.int32, (rows_dev, rows_dev + 2 * HALF_ROWS), 0)
    row_in = lax.broadcasted_iota(jnp.int32, (rows_dev, rows_dev + 2 * HALF_ROWS), 1)
    row_band = ((row_in >= row_out) & (row_in <= row_out + 2 * HALF_ROWS)).astype(jnp.float32)
    col_out = lax.broadcasted_iota(jnp.int32, (columns, columns), 0)
    col_in = lax.broadcasted_iota(jnp.int32, (columns, columns), 1)
    col_band = (jnp.abs(col_out - col_in) <= HALF_COLS).astype(jnp.float32)

    def window(field):
        summed = jnp.einsum("rs,...sc->...rc", row_band, field, precision=HIGH)
        return jnp.einsum("...rc,cd->...rd", summed, col_band, precision=HIGH)

    loc_real = haloed[:, 0]
    loc_imag = haloed[:, 1]
    loc_power = window(loc_real * loc_real + loc_imag * loc_imag)
    piece = lax.all_gather(haloed, "date", axis=0, tiled=True)
    oth_real = piece[:, 0]
    oth_imag = piece[:, 1]
    oth_power = window(oth_real * oth_real + oth_imag * oth_imag)
    cross_real = loc_real[:, None] * oth_real[None] + loc_imag[:, None] * oth_imag[None]
    cross_imag = loc_imag[:, None] * oth_real[None] - loc_real[:, None] * oth_imag[None]
    sums = window(jnp.stack([cross_real, cross_imag], axis=2))
    factor = 1.0 / jnp.sqrt(loc_power[:, None] * oth_power[None] + epsilon)
    in_order = sums * factor[:, :, None]
    coherence = jnp.take(in_order, plan, axis=1)
    return coherence


def solution(mesh):
    placed = (P(("grp", "date"), None, "row", None), P())
    return jax.shard_map(
        body,
        mesh=mesh,
        in_specs=placed,
        out_specs=P(("grp", "date"), None, None, "row", None),
        check_vma=False,
    )
```

profile of v0, /device:TPU:1, one launch (start us, length us, event | category | flops | bytes accessed | tf_op | source)
XLA Modules:
  0.0 34.2 jit_solution(6815068337701900033)
XLA Ops:
  0.0 0.9 %fusion.35 = (f32[2,2,4,512]{3,2,1,0:T(4,128)S(1)}, f32[2,2,4,512]{3,2,1,0:T(4,128)S(1)}) fusion(f32[2,2,16,512]{3,2,1,0:T(8,128)} %param.2), kind=kLoop, calls=%fused_computation.50 | loop fusion | bytes 131072 | tf_op jit(solution)/shard_map/slice | solution.py:19
  0.9 4.5 %collective-permute-start = (f32[2,2,4,512]{3,2,1,0:T(4,128)S(1)}, f32[2,2,4,512]{3,2,1,0:T(4,128)S(1)}, u32[]{:S(2)}, u32[]{:S(2)}) collective-permute-start(f32[2,2,4,512]{3,2,1,0:T(4,128)S(1)} %get-tuple-element.11), channel_id=1, source_target_pairs={{0,1},{1,2},{2,3},{4,5},{5,6},{6,7},{8,9},{9,10},{10,11},{12,13},{... | collective-permute-start | bytes 98312 | tf_op jit(solution)/shard_map/ppermute | solution.py:21
  5.4 1.9 %collective-permute-start.1 = (f32[2,2,4,512]{3,2,1,0:T(4,128)S(1)}, f32[2,2,4,512]{3,2,1,0:T(4,128)S(1)}, u32[]{:S(2)}, u32[]{:S(2)}) collective-permute-start(f32[2,2,4,512]{3,2,1,0:T(4,128)S(1)} %get-tuple-element.12), channel_id=1, source_target_pairs={{1,0},{2,1},{3,2},{5,4},{6,5},{7,6},{9,8},{10,9},{11,10},{13,12},{... | collective-permute-start | bytes 98312 | tf_op jit(solution)/shard_map/ppermute | solution.py:22
  7.3 0.7 %compare_and_fusion = pred[8]{0:T(512)(128)(4,1)S(1)} fusion(s32[8]{0:T(128)} %param.3), kind=kLoop, calls=%fused_computation.44 | loop fusion | flops 48 | bytes 40 | tf_op jit(solution)/shard_map/jit(_take)/and | solution.py:54
  8.0 0.7 %compare_select_fusion = s32[8]{0:T(128)S(1)} fusion(s32[8]{0:T(128)} %param.3), kind=kLoop, calls=%fused_computation.43 | loop fusion | flops 24 | bytes 64 | tf_op jit(solution)/shard_map/jit(_take)/jit(_where)/select_n | solution.py:54
  8.7 0.0 collective-permute-done
  8.7 2.0 %collective-permute-done.1 = f32[2,2,4,512]{3,2,1,0:T(4,128)S(1)} collective-permute-done((f32[2,2,4,512]{3,2,1,0:T(4,128)S(1)}, f32[2,2,4,512]{3,2,1,0:T(4,128)S(1)}, u32[]{:S(2)}, u32[]{:S(2)}) %collective-permute-start.1) | collective-permute-done | bytes 32800 | tf_op jit(solution)/shard_map/ppermute | solution.py:22
  10.6 0.9 %pad_maximum_fusion = f32[2,2,24,512]{3,2,1,0:T(8,128)S(1)} fusion(f32[2,2,4,512]{3,2,1,0:T(4,128)S(1)} %collective-permute-done.1, f32[2,2,16,512]{3,2,1,0:T(8,128)} %param.2, f32[2,2,4,512]{3,2,1,0:T(4,128)S(1)} %collective-permute-done), kind=kLoop, calls=%fused_computation.27 | loop fusion | flops 98304 | bytes 393216 | tf_op jit(solution)/shard_map/concatenate | solution.py:23
  11.6 17.1 %all_gather.3 = f32[8,2,24,512]{3,2,1,0:T(8,128)S(1)} all-gather(f32[2,2,24,512]{3,2,1,0:T(8,128)S(1)} %pad_maximum_fusion), channel_id=1, replica_groups=mesh['grp'=2,'date'=4,'row'=4] {'date'}, dimensions={0}, use_global_device_ids=true | all-gather | bytes 983040 | tf_op jit(solution)/shard_map/all_gather | solution.py:45
  28.7 0.2 convolution_bitcast_fusion.1
  28.9 0.3 convolution_bitcast_fusion
  29.3 0.1 slice_bitcast_fusion.1
  29.4 0.3 fusion.10
  29.7 0.4 %fusion.8 = f32[8,16,512]{2,1,0:T(8,128)S(1)} fusion(f32[8,16,512]{2,1,0:T(8,128)S(1)} %convolution_bitcast_fusion), kind=kOutput, calls=%fused_computation.12 | convolution fusion | flops 403439616 | bytes 524288 | tf_op jit(solution)/shard_map/...rc,cd->...rd/dot_general | solution.py:40
  30.1 0.1 add_rsqrt_fusion
  30.2 0.2 multiply_add_fusion
  30.4 0.8 %fusion.4 = f32[2,8,2,16,512]{4,3,2,1,0:T(8,128)S(1)} fusion(f32[2,8,1,24,512]{4,3,2,1,0:T(8,128)S(1)} %get-tuple-element.6, f32[2,8,1,24,512]{4,3,2,1,0:T(8,128)S(1)} %get-tuple-element.5, s32[16]{0:T(128)S(1)} %iota_add_fusion), kind=kOutput, calls=%fused_computation.5 | convolution fusion | flops 75891840 | bytes 2621504 | tf_op jit(solution)/shard_map/rs,...sc->...rc/dot_general | solution.py:39
  31.3 1.0 %convolution_multiply_fusion = f32[2,8,2,16,512]{4,3,2,1,0:T(8,128)S(1)} fusion(f32[2,8,2,16,512]{4,3,2,1,0:T(8,128)S(1)} %fusion.4, f32[2,8,16,512]{3,2,1,0:T(8,128)S(1)} %add_rsqrt_fusion), kind=kOutput, calls=%fused_computation.6 | convolution fusion | flops 1611661312 | bytes 2621440 | tf_op jit(solution)/shard_map/...rc,cd->...rd/dot_general | solution.py:40
  32.3 0.6 %gather_fusion = f32[8,2,2,16,512]{4,3,2,1,0:T(8,128)S(1)} fusion(f32[2,8,2,16,512]{4,3,2,1,0:T(8,128)S(1)} %convolution_multiply_fusion, s32[1024]{0:T(1024)S(1)} %pad_clamp_fusion), kind=kCustom, calls=%fused_computation | custom fusion | bytes 2097184 | tf_op jit(solution)/shard_map/jit(_take)/gather | solution.py:54
  32.9 0.2 select_bitcast_fusion
  33.1 1.1 %copy.8 = f32[2,8,2,16,512]{4,3,2,1,0:T(8,128)} copy(f32[2,8,2,16,512]{4,3,2,0,1:T(8,128)S(1)} %select_bitcast_fusion) | data formatting | bytes 2097152 | tf_op jit(solution)/shard_map/jit(_take)/select_n | solution.py:54
  (3 shorter events, 0.0 us)
Async XLA Ops:
  0.9 7.8 %collective-permute-start = (f32[2,2,4,512]{3,2,1,0:T(4,128)S(1)}, f32[2,2,4,512]{3,2,1,0:T(4,128)S(1)}, u32[]{:S(2)}, u32[]{:S(2)}) collective-permute-start(f32[2,2,4,512]{3,2,1,0:T(4,128)S(1)} %get-tuple-element.11), channel_id=1, source_target_pairs={{0,1},{1,2},{2,3},{4,5},{5,6},{6,7},{8,9},{9,10},{10,11},{12,13},{... | collective-permute-start | bytes 98312 | tf_op jit(solution)/shard_map/ppermute | solution.py:21
  5.4 5.2 %collective-permute-start.1 = (f32[2,2,4,512]{3,2,1,0:T(4,128)S(1)}, f32[2,2,4,512]{3,2,1,0:T(4,128)S(1)}, u32[]{:S(2)}, u32[]{:S(2)}) collective-permute-start(f32[2,2,4,512]{3,2,1,0:T(4,128)S(1)} %get-tuple-element.12), channel_id=1, source_target_pairs={{1,0},{2,1},{3,2},{5,4},{6,5},{7,6},{9,8},{10,9},{11,10},{13,12},{... | collective-permute-start | bytes 98312 | tf_op jit(solution)/shard_map/ppermute | solution.py:22
where the time goes:
time: 34.4 us; the launch traced here: 34.2 us
  blocking collectives  17.1 us (50%)
  starting transfers between devices  6.42 us (19%)
  matrix products  3.09 us (9%)
  other arithmetic  2.78 us (8%)
  local copies, waits for them, and re-layouts  2.65 us (8%)
  waiting for transfers between devices  1.96 us (6%)
    all_gather x1, blocking collectives, body(): piece = lax.all_gather(haloed, 'date', axis=0, tiled=True)  17.1 us
    ppermute x1, starting transfers between devices, extended(): before = lax.ppermute(last, axis, up)  4.5 us
    ppermute x1, waiting for transfers between devices, extended(): after = lax.ppermute(first, axis, down)  1.96 us
    ppermute x1, starting transfers between devices, extended(): after = lax.ppermute(first, axis, down)  1.92 us
    dot_general x3, matrix products, window(): return jnp.einsum('...rc,cd->...rd', summed, col_band, precision=HIGH)  1.74 us
    dot_general x3, matrix products, window(): summed = jnp.einsum('rs,...sc->...rc', row_band, field, precision=HIGH)  1.35 us
    select_n x1, local copies, waits for them, and re-layouts, body(): coherence = jnp.take(in_order, plan, axis=1)  1.08 us
    concatenate x1, other arithmetic, extended(): array = jnp.concatenate([before, array, after], axis=dim)  0.94 us
  transfers between devices with their start and end apart: 2, of which 1 were waited for; matrix products, arithmetic and copies ran while one was open for 4% of the time, Pallas kernels for 0%

commit v1 on v0

v1 whole, which is shorter than its diff:
```python
import functools

import jax
import jax.numpy as jnp
from jax import lax
from jax.experimental import pallas as pl
from jax.experimental.pallas import tpu as pltpu
from jax.sharding import PartitionSpec as P

HALF_ROWS = 4
HALF_COLS = 16
RIM = 8
LANES = 128

epsilon = 1e-06


def gather_kernel(n, rows_n, x_ref, coh, own, top, bot, band, pbuf, sbuf, lhs, pw,
                  load_sem, unit_recv, right_send, left_send, top_recv, bot_recv, down_send, up_send):
    local, _, height, width = x_ref.shape
    tiles = width // LANES
    me = lax.axis_index("date")
    row = lax.axis_index("row")
    right, left = lax.rem(me + 1, n), lax.rem(me + n - 1, n)
    has_up, has_down = row > 0, row < rows_n - 1
    even = n % 2 == 0
    full = (n - 1) // 2
    half = local // 2

    load = pltpu.make_async_copy(x_ref, own.at[me], load_sem)
    load.start()
    barrier = pltpu.get_barrier_semaphore()

    def greet(axis, index):
        pl.semaphore_signal(barrier, inc=1, device_id={axis: index}, device_id_type=pl.DeviceIdType.MESH)

    if n > 1:
        greet("date", right)
        greet("date", left)
    pl.when(has_up)(lambda: greet("row", row - 1))
    pl.when(has_down)(lambda: greet("row", row + 1))

    col_in = lax.broadcasted_iota(jnp.int32, (width, width), 0)
    col_out = lax.broadcasted_iota(jnp.int32, (width, width), 1)
    band[...] = jnp.where(jnp.abs(col_in - col_out) <= HALF_COLS, 1.0, 0.0).astype(jnp.bfloat16)

    @pl.when(row == 0)
    def _():
        top[...] = jnp.zeros_like(top)

    @pl.when(row == rows_n - 1)
    def _():
        bot[...] = jnp.zeros_like(bot)

    def remote(src, dst, send_sem, recv_sem, axis, index):
        return pltpu.make_async_remote_copy(
            src_ref=src, dst_ref=dst, send_sem=send_sem, recv_sem=recv_sem,
            device_id={axis: index}, device_id_type=pl.DeviceIdType.MESH)

    def to_right(s, l):
        return remote(own.at[s, l], own.at[s, l], right_send.at[s, l], unit_recv.at[s, l], "date", right)

    def to_left(s, l):
        return remote(own.at[s, l], own.at[s, l], left_send.at[s, l], unit_recv.at[s, l], "date", left)

    def to_down(s, l):
        return remote(own.at[s, l, :, pl.ds(height - RIM, RIM)], top.at[s, l], down_send.at[s, l],
                      top_recv.at[s, l], "row", row + 1)

    def to_up(s, l):
        return remote(own.at[s, l, :, pl.ds(0, RIM)], bot.at[s, l], up_send.at[s, l],
                      bot_recv.at[s, l], "row", row - 1)

    def send_rims(s, l):
        pl.when(has_down)(lambda: to_down(s, l).start())
        pl.when(has_up)(lambda: to_up(s, l).start())

    def wait_rims(s, l):
        pl.when(has_up)(lambda: to_down(s, l).wait_recv())
        pl.when(has_down)(lambda: to_up(s, l).wait_recv())

    def wait_rims_sent(s, l):
        pl.when(has_down)(lambda: to_down(s, l).wait_send())
        pl.when(has_up)(lambda: to_up(s, l).wait_send())

    def sample(s, l, part):
        return jnp.concatenate([top[s, l, part], own[s, l, part], bot[s, l, part]], axis=0)

    def window(fields):
        count = len(fields)
        for f, field in enumerate(fields):
            for c in range(tiles):
                pbuf[f, c] = field[:, c * LANES:(c + 1) * LANES]
        for f in range(count):
            sbuf[f] = (pbuf[f, :, 3:height + 11] + pbuf[f, :, 4:height + 12]) + pbuf[f, :, 5:height + 13]
        for f in range(count):
            total = (sbuf[f, :, 1:height + 1] + sbuf[f, :, 4:height + 4]) + sbuf[f, :, 7:height + 7]
            high = total.astype(jnp.bfloat16)
            low = (total - high.astype(jnp.float32)).astype(jnp.bfloat16)
            for c in range(tiles):
                lhs[f * height:(f + 1) * height, c * LANES:(c + 1) * LANES] = high[c]
                lhs[(count + f) * height:(count + f + 1) * height, c * LANES:(c + 1) * LANES] = low[c]
        sums = jnp.dot(lhs[0:2 * count * height], band[...], preferred_element_type=jnp.float32)
        return [sums[f * height:(f + 1) * height] + sums[(count + f) * height:(count + f + 1) * height]
                for f in range(count)]

    def local_power():
        fields = []
        for i in range(local):
            real, imag = sample(me, i, 0), sample(me, i, 1)
            fields.append(real * real + imag * imag)
        for i, power in enumerate(window(fields)):
            pw[i] = power

    def compute(s, l):
        oth_real, oth_imag = sample(s, l, 0), sample(s, l, 1)
        fields = [oth_real * oth_real + oth_imag * oth_imag]
        for i in range(local):
            real, imag = sample(me, i, 0), sample(me, i, 1)
            fields.append(real * oth_real + imag * oth_imag)
            fields.append(imag * oth_real - real * oth_imag)
        sums = window(fields)
        date = s * local + l
        for i in range(local):
            factor = lax.rsqrt(pw[i] * sums[0] + epsilon)
            coh[i, date, 0] = sums[1 + 2 * i] * factor
            coh[i, date, 1] = sums[2 + 2 * i] * factor

    load.wait()
    greeters = (2 if n > 1 else 0) + jnp.where(has_up, 1, 0) + jnp.where(has_down, 1, 0)
    pl.semaphore_wait(barrier, greeters)

    order = [(p, local - 1 - p) for p in range(local)]
    for p, q in order:
        if full >= 1 or (even and p < half):
            to_right(me, p).start()
        if full >= 1 or (even and q >= half):
            to_left(me, q).start()
    for l in range(local):
        send_rims(me, l)
    for l in range(local):
        wait_rims(me, l)
    local_power()
    for l in range(local):
        compute(me, l)

    def sources(t):
        return lax.rem(me + (n - 1) - t, n), lax.rem(me + 1 + t, n)

    def forwards(t, p, q, s_left, s_right, act_right, act_left):
        if even and p < half:
            act_right(s_left, p)
        else:
            pl.when(t < full - 1)(lambda: act_right(s_left, p))
        if even and q >= half:
            act_left(s_right, q)
        else:
            pl.when(t < full - 1)(lambda: act_left(s_right, q))

    def step(t, carry):
        s_left, s_right = sources(t)
        for p, q in order:
            to_right(s_left, p).wait_recv()
            to_left(s_right, q).wait_recv()
            forwards(t, p, q, s_left, s_right, lambda s, l: to_right(s, l).start(),
                     lambda s, l: to_left(s, l).start())
            send_rims(s_left, p)
            send_rims(s_right, q)
        for p, q in order:
            for s, l in ((s_left, p), (s_right, q)):
                wait_rims(s, l)
                compute(s, l)
        return carry

    if full >= 1:
        lax.fori_loop(0, full, step, 0)
    if even:
        far = lax.rem(me + n // 2, n)
        for l in range(local):
            (to_right if l < half else to_left)(far, l).wait_recv()
            send_rims(far, l)
        for l in range(local):
            wait_rims(far, l)
            compute(far, l)

    for p, q in order:
        if full >= 1 or (even and p < half):
            to_right(me, p).wait_send()
        if full >= 1 or (even and q >= half):
            to_left(me, q).wait_send()
    for l in range(local):
        wait_rims_sent(me, l)

    def drain(t, carry):
        s_left, s_right = sources(t)
        for p, q in order:
            forwards(t, p, q, s_left, s_right, lambda s, l: to_right(s, l).wait_send(),
                     lambda s, l: to_left(s, l).wait_send())
            wait_rims_sent(s_left, p)
            wait_rims_sent(s_right, q)
        return carry

    if full >= 1:
        lax.fori_loop(0, full, drain, 0)
    if even:
        for l in range(local):
            wait_rims_sent(far, l)


def order_kernel(plan_ref, coh, out, sem):
    dates = out.shape[1]

    def copy(k):
        return pltpu.make_async_copy(coh.at[:, plan_ref[k]], out.at[:, k], sem.at[k])

    def start(k, carry):
        copy(k).start()
        return carry

    def finish(k, carry):
        copy(k).wait()
        return carry

    lax.fori_loop(0, dates, start, 0)
    lax.fori_loop(0, dates, finish, 0)


def body(n, rows_n, stack_data, plan):
    local, _, height, width = stack_data.shape
    dates = local * n
    tiles = width // LANES
    fields = 2 * local + 1
    kind = jax.ShapeDtypeStruct((local, dates, 2, height, width), jnp.float32)
    dma = pltpu.SemaphoreType.DMA
    result_bytes = local * dates * 2 * height * width * 4
    coh = pl.pallas_call(
        functools.partial(gather_kernel, n, rows_n),
        out_shape=kind,
        in_specs=[pl.BlockSpec(memory_space=pl.ANY)],
        out_specs=pl.BlockSpec(memory_space=pltpu.VMEM),
        scratch_shapes=[
            pltpu.VMEM((n, local, 2, height, width), jnp.float32),
            pltpu.VMEM((n, local, 2, RIM, width), jnp.float32),
            pltpu.VMEM((n, local, 2, RIM, width), jnp.float32),
            pltpu.VMEM((width, width), jnp.bfloat16),
            pltpu.VMEM((fields, tiles, height + 2 * RIM, LANES), jnp.float32),
            pltpu.VMEM((fields, tiles, height + RIM, LANES), jnp.float32),
            pltpu.VMEM((2 * fields * height, width), jnp.bfloat16),
            pltpu.VMEM((local, height, width), jnp.float32),
            dma,
            dma((n, local)), dma((n, local)), dma((n, local)),
            dma((n, local)), dma((n, local)), dma((n, local)), dma((n, local)),
        ],
        compiler_params=pltpu.CompilerParams(
            collective_id=0, has_side_effects=True,
            vmem_limit_bytes=4 * result_bytes + (8 << 20)),
    )(stack_data)
    return pl.pallas_call(
        order_kernel,
        out_shape=kind,
        in_specs=[pl.BlockSpec(memory_space=pltpu.SMEM), pl.BlockSpec(memory_space=pltpu.VMEM)],
        out_specs=pl.BlockSpec(memory_space=pl.ANY),
        scratch_shapes=[dma((dates,))],
        compiler_params=pltpu.CompilerParams(vmem_limit_bytes=2 * result_bytes + (2 << 20)),
    )(plan, coh)


def solution(mesh):
    placed = (P(("grp", "date"), None, "row", None), P())
    return jax.shard_map(
        functools.partial(body, mesh.shape["date"], mesh.shape["row"]),
        mesh=mesh,
        in_specs=placed,
        out_specs=P(("grp", "date"), None, None, "row", None),
        check_vma=False,
    )
```

time: 34.4 us -> 22.3 us (0.65)
  Pallas kernels: 0 us -> 21.3 us
  blocking collectives: 17.1 us -> 0 us
  starting transfers between devices: 6.42 us -> 0 us
  matrix products: 3.09 us -> 0 us
  other arithmetic: 2.78 us -> 0 us
  waiting for transfers between devices: 1.96 us -> 0 us
  local copies, waits for them, and re-layouts: 2.65 us -> 0.91 us
    pallas_call x0 -> x2, Pallas kernels: none -> 21.3 us  [the longest x1 19.7 us: body(): pl.pallas_call(functools.partial(gather_kernel, n, rows_n), out_shape=kin...]
    all_gather x1 -> x0, blocking collectives: 17.1 us -> none  [body(): piece = lax.all_gather(haloed, 'date', axis=0, tiled=True)]
    ppermute x2 -> x0, starting transfers between devices: 6.42 us -> none  [the longest x1 4.5 us: extended(): before = lax.ppermute(last, axis, up)]
    dot_general x6 -> x0, matrix products: 3.09 us -> none  [the longest x3 1.74 us: window(): return jnp.einsum('...rc,cd->...rd', summed, col_band, precision=HIGH)]
    ppermute x2 -> x0, waiting for transfers between devices: 1.96 us -> none  [the longest x1 1.96 us: extended(): after = lax.ppermute(first, axis, down)]
    select_n x1 -> x0, local copies, waits for them, and re-layouts: 1.08 us -> none  [body(): coherence = jnp.take(in_order, plan, axis=1)]
    concatenate x1 -> x0, other arithmetic: 0.94 us -> none  [extended(): array = jnp.concatenate([before, array, after], axis=dim)]
    unnamed x0 -> x4, local copies, waits for them, and re-layouts: none -> 0.91 us
  transfers between devices with their start and end apart: 2 -> 0, of which waited for: 1 -> 0; matrix products, arithmetic and copies ran while one was open for 4% -> 0% of each run, Pallas kernels for 0% -> 0%
where the time goes in v1:
time: 22.3 us; the launch traced here: 22.2 us
  Pallas kernels  21.3 us (96%)
  local copies, waits for them, and re-layouts  0.91 us (4%)
    pallas_call x1, Pallas kernels, body(): pl.pallas_call(functools.partial(gather_kernel, n, rows_n), out_shape=kin...  19.7 us
    pallas_call x1, Pallas kernels, body(): pl.pallas_call(order_kernel, out_shape=kind, in_specs=[pl.BlockSpec(memor...  1.57 us
    unnamed x4, local copies, waits for them, and re-layouts  0.91 us

profile of v1, /device:TPU:1, one launch (start us, length us, event | category | flops | bytes accessed | tf_op | source)
XLA Modules:
  0.0 22.2 jit_solution(944596559373186941)
XLA Ops:
  0.0 0.0 copy-start
  0.0 0.9 %copy-done = f32[2,2,16,512]{3,2,1,0:T(8,128)S(1)} copy-done((f32[2,2,16,512]{3,2,1,0:T(8,128)S(1)}, f32[2,2,16,512]{3,2,1,0:T(8,128)}, u32[]{:S(2)}) %copy-start) | copy-done | bytes 131096
  0.9 0.0 copy-start.1
  0.9 19.7 %shard_map.28.coh = f32[2,8,2,16,512]{4,3,2,1,0:T(8,128)S(1)} custom-call(f32[2,2,16,512]{3,2,1,0:T(8,128)S(1)} %copy-done), custom_call_target="tpu_custom_call" | custom-call | tf_op jit(solution)/shard_map/pallas_call | solution.py:236
  20.6 0.0 copy-done.1
  20.6 1.6 %shard_map.29 = f32[2,8,2,16,512]{4,3,2,1,0:T(8,128)} custom-call(s32[8]{0:T(128)S(1)} %copy-done.1, f32[2,8,2,16,512]{4,3,2,1,0:T(8,128)S(1)} %shard_map.28.coh), custom_call_target="tpu_custom_call" | custom-call | tf_op jit(solution)/shard_map/pallas_call | solution.py:258
Async XLA Ops:
  0.0 0.9 %copy-start = (f32[2,2,16,512]{3,2,1,0:T(8,128)S(1)}, f32[2,2,16,512]{3,2,1,0:T(8,128)}, u32[]{:S(2)}) copy-start(f32[2,2,16,512]{3,2,1,0:T(8,128)} %x_ref.1) | copy-start | bytes 393220
  0.9 19.7 %copy-start.1 = (s32[8]{0:T(128)S(1)}, s32[8]{0:T(128)}, u32[]{:S(2)}) copy-start(s32[8]{0:T(128)} %plan_ref.1) | copy-start | bytes 100

commit v2 on v1

--- a/solution.py
+++ b/solution.py
@@ -11,6 +11,7 @@
 HALF_COLS = 16
 RIM = 8
 LANES = 128
+VMEM_BYTES = 67043328
 
 epsilon = 1e-06
 
@@ -21,11 +22,8 @@
     tiles = width // LANES
     me = lax.axis_index("date")
     row = lax.axis_index("row")
-    right, left = lax.rem(me + 1, n), lax.rem(me + n - 1, n)
+    has_left, has_right = me > 0, me < n - 1
     has_up, has_down = row > 0, row < rows_n - 1
-    even = n % 2 == 0
-    full = (n - 1) // 2
-    half = local // 2
 
     load = pltpu.make_async_copy(x_ref, own.at[me], load_sem)
     load.start()
@@ -34,9 +32,8 @@
     def greet(axis, index):
         pl.semaphore_signal(barrier, inc=1, device_id={axis: index}, device_id_type=pl.DeviceIdType.MESH)
 
-    if n > 1:
-        greet("date", right)
-        greet("date", left)
+    pl.when(has_left)(lambda: greet("date", me - 1))
+    pl.when(has_right)(lambda: greet("date", me + 1))
     pl.when(has_up)(lambda: greet("row", row - 1))
     pl.when(has_down)(lambda: greet("row", row + 1))
 
@@ -58,10 +55,10 @@
             device_id={axis: index}, device_id_type=pl.DeviceIdType.MESH)
 
     def to_right(s, l):
-        return remote(own.at[s, l], own.at[s, l], right_send.at[s, l], unit_recv.at[s, l], "date", right)
+        return remote(own.at[s, l], own.at[s, l], right_send.at[s, l], unit_recv.at[s, l], "date", me + 1)
 
     def to_left(s, l):
-        return remote(own.at[s, l], own.at[s, l], left_send.at[s, l], unit_recv.at[s, l], "date", left)
+        return remote(own.at[s, l], own.at[s, l], left_send.at[s, l], unit_recv.at[s, l], "date", me - 1)
 
     def to_down(s, l):
         return remote(own.at[s, l, :, pl.ds(height - RIM, RIM)], top.at[s, l], down_send.at[s, l],
@@ -127,16 +124,12 @@
             coh[i, date, 1] = sums[2 + 2 * i] * factor
 
     load.wait()
-    greeters = (2 if n > 1 else 0) + jnp.where(has_up, 1, 0) + jnp.where(has_down, 1, 0)
+    greeters = functools.reduce(jnp.add, [jnp.where(near, 1, 0) for near in (has_left, has_right, has_up, has_down)])
     pl.semaphore_wait(barrier, greeters)
 
-    order = [(p, local - 1 - p) for p in range(local)]
-    for p, q in order:
-        if full >= 1 or (even and p < half):
-            to_right(me, p).start()
-        if full >= 1 or (even and q >= half):
-            to_left(me, q).start()
-    for l in range(local):
+    for l in range(local):
+        pl.when(has_right)(lambda l=l: to_right(me, l).start())
+        pl.when(has_left)(lambda l=l: to_left(me, l).start())
         send_rims(me, l)
     for l in range(local):
         wait_rims(me, l)
@@ -144,67 +137,59 @@
     for l in range(local):
         compute(me, l)
 
-    def sources(t):
-        return lax.rem(me + (n - 1) - t, n), lax.rem(me + 1 + t, n)
-
-    def forwards(t, p, q, s_left, s_right, act_right, act_left):
-        if even and p < half:
-            act_right(s_left, p)
-        else:
-            pl.when(t < full - 1)(lambda: act_right(s_left, p))
-        if even and q >= half:
-            act_left(s_right, q)
-        else:
-            pl.when(t < full - 1)(lambda: act_left(s_right, q))
-
-    def step(t, carry):
-        s_left, s_right = sources(t)
-        for p, q in order:
-            to_right(s_left, p).wait_recv()
-            to_left(s_right, q).wait_recv()
-            forwards(t, p, q, s_left, s_right, lambda s, l: to_right(s, l).start(),
-                     lambda s, l: to_left(s, l).start())
-            send_rims(s_left, p)
-            send_rims(s_right, q)
-        for p, q in order:
-            for s, l in ((s_left, p), (s_right, q)):
+    def finish(t, l):
+        for s, there in ((me - 1 - t, me - 1 - t >= 0), (me + 1 + t, me + 1 + t < n)):
+            @pl.when(there)
+            def _(s=s):
                 wait_rims(s, l)
                 compute(s, l)
-        return carry
-
-    if full >= 1:
-        lax.fori_loop(0, full, step, 0)
-    if even:
-        far = lax.rem(me + n // 2, n)
+
+    def step(t, carry):
+        s_left, s_right = me - 1 - t, me + 1 + t
         for l in range(local):
-            (to_right if l < half else to_left)(far, l).wait_recv()
-            send_rims(far, l)
+            @pl.when(s_left >= 0)
+            def _():
+                to_right(s_left, l).wait_recv()
+                pl.when(has_right)(lambda: to_right(s_left, l).start())
+                send_rims(s_left, l)
+
+            @pl.when(s_right < n)
+            def _():
+                to_left(s_right, l).wait_recv()
+                pl.when(has_left)(lambda: to_left(s_right, l).start())
+                send_rims(s_right, l)
+
+            if l > 0:
+                finish(t, l - 1)
+            else:
+                pl.when(t > 0)(lambda: finish(t - 1, local - 1))
+        return carry
+
+    if n > 1:
+        lax.fori_loop(0, n - 1, step, 0)
+        finish(n - 2, local - 1)
+
+    for l in range(local):
+        pl.when(has_right)(lambda l=l: to_right(me, l).wait_send())
+        pl.when(has_left)(lambda l=l: to_left(me, l).wait_send())
+        wait_rims_sent(me, l)
+
+    def drain(t, carry):
+        s_left, s_right = me - 1 - t, me + 1 + t
         for l in range(local):
-            wait_rims(far, l)
-            compute(far, l)
-
-    for p, q in order:
-        if full >= 1 or (even and p < half):
-            to_right(me, p).wait_send()
-        if full >= 1 or (even and q >= half):
-            to_left(me, q).wait_send()
-    for l in range(local):
-        wait_rims_sent(me, l)
-
-    def drain(t, carry):
-        s_left, s_right = sources(t)
-        for p, q in order:
-            forwards(t, p, q, s_left, s_right, lambda s, l: to_right(s, l).wait_send(),
-                     lambda s, l: to_left(s, l).wait_send())
-            wait_rims_sent(s_left, p)
-            wait_rims_sent(s_right, q)
-        return carry
-
-    if full >= 1:
-        lax.fori_loop(0, full, drain, 0)
-    if even:
-        for l in range(local):
-            wait_rims_sent(far, l)
+            @pl.when(s_left >= 0)
+            def _():
+                pl.when(has_right)(lambda: to_right(s_left, l).wait_send())
+                wait_rims_sent(s_left, l)
+
+            @pl.when(s_right < n)
+            def _():
+                pl.when(has_left)(lambda: to_left(s_right, l).wait_send())
+                wait_rims_sent(s_right, l)
+        return carry
+
+    if n > 1:
+        lax.fori_loop(0, n - 1, drain, 0)
 
 
 def order_kernel(plan_ref, coh, out, sem):
@@ -236,7 +221,7 @@
     coh = pl.pallas_call(
         functools.partial(gather_kernel, n, rows_n),
         out_shape=kind,
-        in_specs=[pl.BlockSpec(memory_space=pl.ANY)],
+        in_specs=[pl.BlockSpec(memory_space=pltpu.HBM)],
         out_specs=pl.BlockSpec(memory_space=pltpu.VMEM),
         scratch_shapes=[
             pltpu.VMEM((n, local, 2, height, width), jnp.float32),
@@ -253,7 +238,7 @@
         ],
         compiler_params=pltpu.CompilerParams(
             collective_id=0, has_side_effects=True,
-            vmem_limit_bytes=4 * result_bytes + (8 << 20)),
+            vmem_limit_bytes=VMEM_BYTES - result_bytes - 2 * stack_data.size),
     )(stack_data)
     return pl.pallas_call(
         order_kernel,

time: 22.3 us -> 22.7 us (1.018)
  local copies, waits for them, and re-layouts: 0.91 us -> 1.22 us
    unnamed x4, local copies, waits for them, and re-layouts: 0.91 us -> 1.22 us
where the time goes in v2:
time: 22.7 us; the launch traced here: 22.5 us
  Pallas kernels  21.3 us (94%)
  local copies, waits for them, and re-layouts  1.22 us (5%)
    pallas_call x1, Pallas kernels, body(): pl.pallas_call(functools.partial(gather_kernel, n, rows_n), out_shape=kin...  19.7 us
    pallas_call x1, Pallas kernels, body(): pl.pallas_call(order_kernel, out_shape=kind, in_specs=[pl.BlockSpec(memor...  1.57 us
    unnamed x4, local copies, waits for them, and re-layouts  1.22 us

profile of v2, /device:TPU:1, one launch (start us, length us, event | category | flops | bytes accessed | tf_op | source)
XLA Modules:
  0.0 22.5 jit_solution(10752524285137996260)
XLA Ops:
  0.0 0.0 copy-start.1
  0.0 19.7 %shard_map.28.coh = f32[2,8,2,16,512]{4,3,2,1,0:T(8,128)} custom-call(f32[2,2,16,512]{3,2,1,0:T(8,128)} %x_ref.1), custom_call_target="tpu_custom_call" | custom-call | tf_op jit(solution)/shard_map/pallas_call | solution.py:221
  19.7 0.0 copy-done.1
  19.7 0.0 copy-start
  19.7 1.2 %copy-done = f32[2,8,2,16,512]{4,3,2,1,0:T(8,128)S(1)} copy-done((f32[2,8,2,16,512]{4,3,2,1,0:T(8,128)S(1)}, f32[2,8,2,16,512]{4,3,2,1,0:T(8,128)}, u32[]{:S(2)}) %copy-start) | copy-done | bytes 1048600
  21.0 1.6 %shard_map.29 = f32[2,8,2,16,512]{4,3,2,1,0:T(8,128)} custom-call(s32[8]{0:T(128)S(1)} %copy-done.1, f32[2,8,2,16,512]{4,3,2,1,0:T(8,128)S(1)} %copy-done), custom_call_target="tpu_custom_call" | custom-call | tf_op jit(solution)/shard_map/pallas_call | solution.py:243
Async XLA Ops:
  0.0 19.7 %copy-start.1 = (s32[8]{0:T(128)S(1)}, s32[8]{0:T(128)}, u32[]{:S(2)}) copy-start(s32[8]{0:T(128)} %plan_ref.1) | copy-start | bytes 100
  19.7 1.2 %copy-start = (f32[2,8,2,16,512]{4,3,2,1,0:T(8,128)S(1)}, f32[2,8,2,16,512]{4,3,2,1,0:T(8,128)}, u32[]{:S(2)}) copy-start(f32[2,8,2,16,512]{4,3,2,1,0:T(8,128)} %shard_map.28.coh) | copy-start | bytes 3145732

commit v3 on v2

--- a/solution.py
+++ b/solution.py
@@ -11,7 +11,6 @@
 HALF_COLS = 16
 RIM = 8
 LANES = 128
-VMEM_BYTES = 67043328
 
 epsilon = 1e-06
 
@@ -218,6 +217,7 @@
     kind = jax.ShapeDtypeStruct((local, dates, 2, height, width), jnp.float32)
     dma = pltpu.SemaphoreType.DMA
     result_bytes = local * dates * 2 * height * width * 4
+    stack_data = pltpu.with_memory_space_constraint(stack_data, pltpu.HBM)
     coh = pl.pallas_call(
         functools.partial(gather_kernel, n, rows_n),
         out_shape=kind,
@@ -238,7 +238,7 @@
         ],
         compiler_params=pltpu.CompilerParams(
             collective_id=0, has_side_effects=True,
-            vmem_limit_bytes=VMEM_BYTES - result_bytes - 2 * stack_data.size),
+            vmem_limit_bytes=4 * result_bytes + (8 << 20)),
     )(stack_data)
     return pl.pallas_call(
         order_kernel,

time: 22.7 us -> 20.5 us (0.903)
  local copies, waits for them, and re-layouts: 1.22 us -> 0.01 us
  Pallas kernels: 21.3 us -> 20.3 us
    unnamed x4 -> x2, local copies, waits for them, and re-layouts: 1.22 us -> 0.01 us
    pallas_call x1, Pallas kernels: 19.7 us -> 18.7 us  [body(): pl.pallas_call(functools.partial(gather_kernel, n, rows_n), out_shape=kin...]
where the time goes in v3:
time: 20.5 us; the launch traced here: 20.3 us
  Pallas kernels  20.3 us (99%)
    pallas_call x1, Pallas kernels, body(): pl.pallas_call(functools.partial(gather_kernel, n, rows_n), out_shape=kin...  18.7 us
    pallas_call x1, Pallas kernels, body(): pl.pallas_call(order_kernel, out_shape=kind, in_specs=[pl.BlockSpec(memor...  1.57 us

profile of v3, /device:TPU:1, one launch (start us, length us, event | category | flops | bytes accessed | tf_op | source)
XLA Modules:
  0.0 20.3 jit_solution(294115865578081981)
XLA Ops:
  0.0 0.0 copy-start
  0.0 18.7 %shard_map.28.coh = f32[2,8,2,16,512]{4,3,2,1,0:T(8,128)S(1)} custom-call(f32[2,2,16,512]{3,2,1,0:T(8,128)} %x_ref.1), custom_call_target="tpu_custom_call" | custom-call | tf_op jit(solution)/shard_map/pallas_call | solution.py:221
  18.7 0.0 copy-done
  18.8 1.6 %shard_map.29 = f32[2,8,2,16,512]{4,3,2,1,0:T(8,128)} custom-call(s32[8]{0:T(128)S(1)} %copy-done, f32[2,8,2,16,512]{4,3,2,1,0:T(8,128)S(1)} %shard_map.28.coh), custom_call_target="tpu_custom_call" | custom-call | tf_op jit(solution)/shard_map/pallas_call | solution.py:243
Async XLA Ops:
  0.0 18.7 %copy-start = (s32[8]{0:T(128)S(1)}, s32[8]{0:T(128)}, u32[]{:S(2)}) copy-start(s32[8]{0:T(128)} %plan_ref.1) | copy-start | bytes 100

commit v4 on v3

--- a/solution.py
+++ b/solution.py
@@ -9,22 +9,23 @@
 
 HALF_ROWS = 4
 HALF_COLS = 16
-RIM = 8
 LANES = 128
 
 epsilon = 1e-06
 
 
-def gather_kernel(n, rows_n, x_ref, coh, own, top, bot, band, pbuf, sbuf, lhs, pw,
-                  load_sem, unit_recv, right_send, left_send, top_recv, bot_recv, down_send, up_send):
+def gather_kernel(n, rows_n, x_ref, coh, own, edge, mid, top, bot, mine, other, band, pbuf, sbuf, lhs, pw,
+                  load_sem, recv, right_send, left_send, top_recv, bot_recv, down_send, up_send):
     local, _, height, width = x_ref.shape
     tiles = width // LANES
+    inner = height - 2 * HALF_ROWS
+    span = height + 2 * HALF_ROWS
     me = lax.axis_index("date")
     row = lax.axis_index("row")
     has_left, has_right = me > 0, me < n - 1
     has_up, has_down = row > 0, row < rows_n - 1
 
-    load = pltpu.make_async_copy(x_ref, own.at[me], load_sem)
+    load = pltpu.make_async_copy(x_ref, own, load_sem)
     load.start()
     barrier = pltpu.get_barrier_semaphore()
 
@@ -53,19 +54,23 @@
             src_ref=src, dst_ref=dst, send_sem=send_sem, recv_sem=recv_sem,
             device_id={axis: index}, device_id_type=pl.DeviceIdType.MESH)
 
-    def to_right(s, l):
-        return remote(own.at[s, l], own.at[s, l], right_send.at[s, l], unit_recv.at[s, l], "date", me + 1)
-
-    def to_left(s, l):
-        return remote(own.at[s, l], own.at[s, l], left_send.at[s, l], unit_recv.at[s, l], "date", me - 1)
+    chunks = [(0, l) for l in range(local)] + [(1, l) for l in range(local)]
+
+    def to_date(sends, step, k, s, l):
+        ref = (edge, mid)[k].at[s, l]
+        return remote(ref, ref, sends.at[k, s, l], recv.at[k, s, l], "date", me + step)
+
+    def to_right(k, s, l):
+        return to_date(right_send, 1, k, s, l)
+
+    def to_left(k, s, l):
+        return to_date(left_send, -1, k, s, l)
 
     def to_down(s, l):
-        return remote(own.at[s, l, :, pl.ds(height - RIM, RIM)], top.at[s, l], down_send.at[s, l],
-                      top_recv.at[s, l], "row", row + 1)
+        return remote(edge.at[s, l, 1], top.at[s, l], down_send.at[s, l], top_recv.at[s, l], "row", row + 1)
 
     def to_up(s, l):
-        return remote(own.at[s, l, :, pl.ds(0, RIM)], bot.at[s, l], up_send.at[s, l],
-                      bot_recv.at[s, l], "row", row - 1)
+        return remote(edge.at[s, l, 0], bot.at[s, l], up_send.at[s, l], bot_recv.at[s, l], "row", row - 1)
 
     def send_rims(s, l):
         pl.when(has_down)(lambda: to_down(s, l).start())
@@ -79,18 +84,25 @@
         pl.when(has_down)(lambda: to_down(s, l).wait_send())
         pl.when(has_up)(lambda: to_up(s, l).wait_send())
 
-    def sample(s, l, part):
-        return jnp.concatenate([top[s, l, part], own[s, l, part], bot[s, l, part]], axis=0)
+    def assemble(dst, s, l):
+        low = height + HALF_ROWS
+        for part in range(2):
+            for c in range(tiles):
+                lanes = slice(c * LANES, (c + 1) * LANES)
+                dst[part, c, 0:HALF_ROWS] = top[s, l, part, :, lanes]
+                dst[part, c, HALF_ROWS:2 * HALF_ROWS] = edge[s, l, 0, part, :, lanes]
+                dst[part, c, 2 * HALF_ROWS:2 * HALF_ROWS + inner] = mid[s, l, part, :, lanes]
+                dst[part, c, height:low] = edge[s, l, 1, part, :, lanes]
+                dst[part, c, low:low + HALF_ROWS] = bot[s, l, part, :, lanes]
 
     def window(fields):
         count = len(fields)
         for f, field in enumerate(fields):
-            for c in range(tiles):
-                pbuf[f, c] = field[:, c * LANES:(c + 1) * LANES]
+            pbuf[f] = field
         for f in range(count):
-            sbuf[f] = (pbuf[f, :, 3:height + 11] + pbuf[f, :, 4:height + 12]) + pbuf[f, :, 5:height + 13]
+            sbuf[f, :, 0:span - 2] = (pbuf[f, :, 0:span - 2] + pbuf[f, :, 1:span - 1]) + pbuf[f, :, 2:span]
         for f in range(count):
-            total = (sbuf[f, :, 1:height + 1] + sbuf[f, :, 4:height + 4]) + sbuf[f, :, 7:height + 7]
+            total = (sbuf[f, :, 0:height] + sbuf[f, :, 3:height + 3]) + sbuf[f, :, 6:height + 6]
             high = total.astype(jnp.bfloat16)
             low = (total - high.astype(jnp.float32)).astype(jnp.bfloat16)
             for c in range(tiles):
@@ -103,16 +115,15 @@
     def local_power():
         fields = []
         for i in range(local):
-            real, imag = sample(me, i, 0), sample(me, i, 1)
+            real, imag = mine[i, 0], mine[i, 1]
             fields.append(real * real + imag * imag)
         for i, power in enumerate(window(fields)):
             pw[i] = power
 
-    def compute(s, l):
-        oth_real, oth_imag = sample(s, l, 0), sample(s, l, 1)
+    def compute(s, l, oth_real, oth_imag):
         fields = [oth_real * oth_real + oth_imag * oth_imag]
         for i in range(local):
-            real, imag = sample(me, i, 0), sample(me, i, 1)
+            real, imag = mine[i, 0], mine[i, 1]
             fields.append(real * oth_real + imag * oth_imag)
             fields.append(imag * oth_real - real * oth_imag)
         sums = window(fields)
@@ -123,44 +134,53 @@
             coh[i, date, 1] = sums[2 + 2 * i] * factor
 
     load.wait()
+    for l in range(local):
+        edge[me, l, 0] = own[l, :, 0:HALF_ROWS]
+        edge[me, l, 1] = own[l, :, height - HALF_ROWS:height]
+        mid[me, l] = own[l, :, HALF_ROWS:height - HALF_ROWS]
     greeters = functools.reduce(jnp.add, [jnp.where(near, 1, 0) for near in (has_left, has_right, has_up, has_down)])
     pl.semaphore_wait(barrier, greeters)
 
-    for l in range(local):
-        pl.when(has_right)(lambda l=l: to_right(me, l).start())
-        pl.when(has_left)(lambda l=l: to_left(me, l).start())
-        send_rims(me, l)
+    for k, l in chunks:
+        pl.when(has_right)(lambda: to_right(k, me, l).start())
+        pl.when(has_left)(lambda: to_left(k, me, l).start())
+        if k == 0:
+            send_rims(me, l)
     for l in range(local):
         wait_rims(me, l)
+        assemble(mine.at[l], me, l)
     local_power()
     for l in range(local):
-        compute(me, l)
+        compute(me, l, mine[l, 0], mine[l, 1])
 
     def finish(t, l):
         for s, there in ((me - 1 - t, me - 1 - t >= 0), (me + 1 + t, me + 1 + t < n)):
             @pl.when(there)
             def _(s=s):
                 wait_rims(s, l)
-                compute(s, l)
+                assemble(other, s, l)
+                compute(s, l, other[0], other[1])
 
     def step(t, carry):
         s_left, s_right = me - 1 - t, me + 1 + t
-        for l in range(local):
+        for k, l in chunks:
             @pl.when(s_left >= 0)
             def _():
-                to_right(s_left, l).wait_recv()
-                pl.when(has_right)(lambda: to_right(s_left, l).start())
-                send_rims(s_left, l)
+                to_right(k, s_left, l).wait_recv()
+                pl.when(has_right)(lambda: to_right(k, s_left, l).start())
+                if k == 0:
+                    send_rims(s_left, l)
 
             @pl.when(s_right < n)
             def _():
-                to_left(s_right, l).wait_recv()
-                pl.when(has_left)(lambda: to_left(s_right, l).start())
-                send_rims(s_right, l)
-
-            if l > 0:
+                to_left(k, s_right, l).wait_recv()
+                pl.when(has_left)(lambda: to_left(k, s_right, l).start())
+                if k == 0:
+                    send_rims(s_right, l)
+
+            if k == 1 and l > 0:
                 finish(t, l - 1)
-            else:
+            if k == 0 and l == 0:
                 pl.when(t > 0)(lambda: finish(t - 1, local - 1))
         return carry
 
@@ -168,23 +188,26 @@
         lax.fori_loop(0, n - 1, step, 0)
         finish(n - 2, local - 1)
 
-    for l in range(local):
-        pl.when(has_right)(lambda l=l: to_right(me, l).wait_send())
-        pl.when(has_left)(lambda l=l: to_left(me, l).wait_send())
-        wait_rims_sent(me, l)
+    for k, l in chunks:
+        pl.when(has_right)(lambda: to_right(k, me, l).wait_send())
+        pl.when(has_left)(lambda: to_left(k, me, l).wait_send())
+        if k == 0:
+            wait_rims_sent(me, l)
 
     def drain(t, carry):
         s_left, s_right = me - 1 - t, me + 1 + t
-        for l in range(local):
+        for k, l in chunks:
             @pl.when(s_left >= 0)
             def _():
-                pl.when(has_right)(lambda: to_right(s_left, l).wait_send())
-                wait_rims_sent(s_left, l)
+                pl.when(has_right)(lambda: to_right(k, s_left, l).wait_send())
+                if k == 0:
+                    wait_rims_sent(s_left, l)
 
             @pl.when(s_right < n)
             def _():
-                pl.when(has_left)(lambda: to_left(s_right, l).wait_send())
-                wait_rims_sent(s_right, l)
+                pl.when(has_left)(lambda: to_left(k, s_right, l).wait_send())
+                if k == 0:
+                    wait_rims_sent(s_right, l)
         return carry
 
     if n > 1:
@@ -214,6 +237,7 @@
     dates = local * n
     tiles = width // LANES
     fields = 2 * local + 1
+    span = height + 2 * HALF_ROWS
     kind = jax.ShapeDtypeStruct((local, dates, 2, height, width), jnp.float32)
     dma = pltpu.SemaphoreType.DMA
     result_bytes = local * dates * 2 * height * width * 4
@@ -224,16 +248,20 @@
         in_specs=[pl.BlockSpec(memory_space=pltpu.HBM)],
         out_specs=pl.BlockSpec(memory_space=pltpu.VMEM),
         scratch_shapes=[
-            pltpu.VMEM((n, local, 2, height, width), jnp.float32),
-            pltpu.VMEM((n, local, 2, RIM, width), jnp.float32),
-            pltpu.VMEM((n, local, 2, RIM, width), jnp.float32),
+            pltpu.VMEM((local, 2, height, width), jnp.float32),
+            pltpu.VMEM((n, local, 2, 2, HALF_ROWS, width), jnp.float32),
+            pltpu.VMEM((n, local, 2, height - 2 * HALF_ROWS, width), jnp.float32),
+            pltpu.VMEM((n, local, 2, HALF_ROWS, width), jnp.float32),
+            pltpu.VMEM((n, local, 2, HALF_ROWS, width), jnp.float32),
+            pltpu.VMEM((local, 2, tiles, span, LANES), jnp.float32),
+            pltpu.VMEM((2, tiles, span, LANES), jnp.float32),
             pltpu.VMEM((width, width), jnp.bfloat16),
-            pltpu.VMEM((fields, tiles, height + 2 * RIM, LANES), jnp.float32),
-            pltpu.VMEM((fields, tiles, height + RIM, LANES), jnp.float32),
+            pltpu.VMEM((fields, tiles, span, LANES), jnp.float32),
+            pltpu.VMEM((fields, tiles, span, LANES), jnp.float32),
             pltpu.VMEM((2 * fields * height, width), jnp.bfloat16),
             pltpu.VMEM((local, height, width), jnp.float32),
             dma,
-            dma((n, local)), dma((n, local)), dma((n, local)),
+            dma((2, n, local)), dma((2, n, local)), dma((2, n, local)),
             dma((n, local)), dma((n, local)), dma((n, local)), dma((n, local)),
         ],
         compiler_params=pltpu.CompilerParams(

time: 20.5 us -> 19.5 us (0.951)
  Pallas kernels: 20.3 us -> 19.3 us
    pallas_call x1, Pallas kernels: 18.7 us -> 17.8 us  [body(): pl.pallas_call(functools.partial(gather_kernel, n, rows_n), out_shape=kin...]
where the time goes in v4:
time: 19.5 us; the launch traced here: 19.3 us
  Pallas kernels  19.3 us (99%)
    pallas_call x1, Pallas kernels, body(): pl.pallas_call(functools.partial(gather_kernel, n, rows_n), out_shape=kin...  17.8 us
    pallas_call x1, Pallas kernels, body(): pl.pallas_call(order_kernel, out_shape=kind, in_specs=[pl.BlockSpec(memor...  1.57 us

profile of v4, /device:TPU:1, one launch (start us, length us, event | category | flops | bytes accessed | tf_op | source)
XLA Modules:
  0.0 19.3 jit_solution(9666538425742625240)
XLA Ops:
  0.0 0.0 copy-start
  0.0 17.8 %shard_map.28.coh = f32[2,8,2,16,512]{4,3,2,1,0:T(8,128)S(1)} custom-call(f32[2,2,16,512]{3,2,1,0:T(8,128)} %x_ref.1), custom_call_target="tpu_custom_call" | custom-call | tf_op jit(solution)/shard_map/pallas_call | solution.py:245
  17.8 0.0 copy-done
  17.8 1.6 %shard_map.29 = f32[2,8,2,16,512]{4,3,2,1,0:T(8,128)} custom-call(s32[8]{0:T(128)S(1)} %copy-done, f32[2,8,2,16,512]{4,3,2,1,0:T(8,128)S(1)} %shard_map.28.coh), custom_call_target="tpu_custom_call" | custom-call | tf_op jit(solution)/shard_map/pallas_call | solution.py:271
Async XLA Ops:
  0.0 17.8 %copy-start = (s32[8]{0:T(128)S(1)}, s32[8]{0:T(128)}, u32[]{:S(2)}) copy-start(s32[8]{0:T(128)} %plan_ref.1) | copy-start | bytes 100

commit v5 on v4

--- a/solution.py
+++ b/solution.py
@@ -146,12 +146,13 @@
         pl.when(has_left)(lambda: to_left(k, me, l).start())
         if k == 0:
             send_rims(me, l)
-    for l in range(local):
-        wait_rims(me, l)
-        assemble(mine.at[l], me, l)
-    local_power()
-    for l in range(local):
-        compute(me, l, mine[l, 0], mine[l, 1])
+    def own_dates():
+        for l in range(local):
+            wait_rims(me, l)
+            assemble(mine.at[l], me, l)
+        local_power()
+        for l in range(local):
+            compute(me, l, mine[l, 0], mine[l, 1])
 
     def finish(t, l):
         for s, there in ((me - 1 - t, me - 1 - t >= 0), (me + 1 + t, me + 1 + t < n)):
@@ -178,15 +179,16 @@
                 if k == 0:
                     send_rims(s_right, l)
 
-            if k == 1 and l > 0:
-                finish(t, l - 1)
-            if k == 0 and l == 0:
-                pl.when(t > 0)(lambda: finish(t - 1, local - 1))
+            if k == 0 and l == local - 1:
+                pl.when(t == 0)(own_dates)
+            if k == 1:
+                finish(t, l)
         return carry
 
     if n > 1:
         lax.fori_loop(0, n - 1, step, 0)
-        finish(n - 2, local - 1)
+    else:
+        own_dates()
 
     for k, l in chunks:
         pl.when(has_right)(lambda: to_right(k, me, l).wait_send())

time: 19.5 us -> 19.3 us (0.990)
  Pallas kernels: 19.3 us -> 19.1 us
where the time goes in v5:
time: 19.3 us; the launch traced here: 19.2 us
  Pallas kernels  19.1 us (99%)
    pallas_call x1, Pallas kernels, body(): pl.pallas_call(functools.partial(gather_kernel, n, rows_n), out_shape=kin...  17.6 us
    pallas_call x1, Pallas kernels, body(): pl.pallas_call(order_kernel, out_shape=kind, in_specs=[pl.BlockSpec(memor...  1.57 us

profile of v5, /device:TPU:1, one launch (start us, length us, event | category | flops | bytes accessed | tf_op | source)
XLA Modules:
  0.0 19.2 jit_solution(6702874982326852137)
XLA Ops:
  0.0 0.0 copy-start
  0.0 17.6 %shard_map.28.coh = f32[2,8,2,16,512]{4,3,2,1,0:T(8,128)S(1)} custom-call(f32[2,2,16,512]{3,2,1,0:T(8,128)} %x_ref.1), custom_call_target="tpu_custom_call" | custom-call | tf_op jit(solution)/shard_map/pallas_call | solution.py:247
  17.6 0.0 copy-done
  17.6 1.6 %shard_map.29 = f32[2,8,2,16,512]{4,3,2,1,0:T(8,128)} custom-call(s32[8]{0:T(128)S(1)} %copy-done, f32[2,8,2,16,512]{4,3,2,1,0:T(8,128)S(1)} %shard_map.28.coh), custom_call_target="tpu_custom_call" | custom-call | tf_op jit(solution)/shard_map/pallas_call | solution.py:273
Async XLA Ops:
  0.0 17.6 %copy-start = (s32[8]{0:T(128)S(1)}, s32[8]{0:T(128)}, u32[]{:S(2)}) copy-start(s32[8]{0:T(128)} %plan_ref.1) | copy-start | bytes 100

commit v6 on v5

--- a/solution.py
+++ b/solution.py
@@ -23,6 +23,7 @@
     me = lax.axis_index("date")
     row = lax.axis_index("row")
     has_left, has_right = me > 0, me < n - 1
+    at_end = jnp.logical_not(jnp.logical_and(has_left, has_right))
     has_up, has_down = row > 0, row < rows_n - 1
 
     load = pltpu.make_async_copy(x_ref, own, load_sem)
@@ -180,13 +181,24 @@
                     send_rims(s_right, l)
 
             if k == 0 and l == local - 1:
-                pl.when(t == 0)(own_dates)
+                pl.when(jnp.logical_and(at_end, t == 0))(own_dates)
             if k == 1:
-                finish(t, l)
+                pl.when(at_end)(lambda: finish(t, l))
         return carry
 
     if n > 1:
         lax.fori_loop(0, n - 1, step, 0)
+
+        @pl.when(jnp.logical_not(at_end))
+        def _():
+            own_dates()
+
+            def late(t, carry):
+                for l in range(local):
+                    finish(t, l)
+                return carry
+
+            lax.fori_loop(0, n - 1, late, 0)
     else:
         own_dates()
 

time: 19.3 us -> 19.1 us (0.990)
  no operation moved by 1% of the time
where the time goes in v6:
time: 19.1 us; the launch traced here: 19 us
  Pallas kernels  19 us (99%)
    pallas_call x1, Pallas kernels, body(): pl.pallas_call(functools.partial(gather_kernel, n, rows_n), out_shape=kin...  17.4 us
    pallas_call x1, Pallas kernels, body(): pl.pallas_call(order_kernel, out_shape=kind, in_specs=[pl.BlockSpec(memor...  1.57 us

profile of v6, /device:TPU:1, one launch (start us, length us, event | category | flops | bytes accessed | tf_op | source)
XLA Modules:
  0.0 19.0 jit_solution(7746311427511381973)
XLA Ops:
  0.0 0.0 copy-start
  0.0 17.4 %shard_map.28.coh = f32[2,8,2,16,512]{4,3,2,1,0:T(8,128)S(1)} custom-call(f32[2,2,16,512]{3,2,1,0:T(8,128)} %x_ref.1), custom_call_target="tpu_custom_call" | custom-call | tf_op jit(solution)/shard_map/pallas_call | solution.py:259
  17.4 0.0 copy-done
  17.4 1.6 %shard_map.29 = f32[2,8,2,16,512]{4,3,2,1,0:T(8,128)} custom-call(s32[8]{0:T(128)S(1)} %copy-done, f32[2,8,2,16,512]{4,3,2,1,0:T(8,128)S(1)} %shard_map.28.coh), custom_call_target="tpu_custom_call" | custom-call | tf_op jit(solution)/shard_map/pallas_call | solution.py:285
Async XLA Ops:
  0.0 17.4 %copy-start = (s32[8]{0:T(128)S(1)}, s32[8]{0:T(128)}, u32[]{:S(2)}) copy-start(s32[8]{0:T(128)} %plan_ref.1) | copy-start | bytes 100

commit v7 on v6

--- a/solution.py
+++ b/solution.py
@@ -37,18 +37,6 @@
     pl.when(has_right)(lambda: greet("date", me + 1))
     pl.when(has_up)(lambda: greet("row", row - 1))
     pl.when(has_down)(lambda: greet("row", row + 1))
-
-    col_in = lax.broadcasted_iota(jnp.int32, (width, width), 0)
-    col_out = lax.broadcasted_iota(jnp.int32, (width, width), 1)
-    band[...] = jnp.where(jnp.abs(col_in - col_out) <= HALF_COLS, 1.0, 0.0).astype(jnp.bfloat16)
-
-    @pl.when(row == 0)
-    def _():
-        top[...] = jnp.zeros_like(top)
-
-    @pl.when(row == rows_n - 1)
-    def _():
-        bot[...] = jnp.zeros_like(bot)
 
     def remote(src, dst, send_sem, recv_sem, axis, index):
         return pltpu.make_async_remote_copy(
@@ -143,10 +131,22 @@
     pl.semaphore_wait(barrier, greeters)
 
     for k, l in chunks:
+        pl.when(has_left)(lambda: to_left(k, me, l).start())
         pl.when(has_right)(lambda: to_right(k, me, l).start())
-        pl.when(has_left)(lambda: to_left(k, me, l).start())
         if k == 0:
             send_rims(me, l)
+    col_in = lax.broadcasted_iota(jnp.int32, (width, width), 0)
+    col_out = lax.broadcasted_iota(jnp.int32, (width, width), 1)
+    band[...] = jnp.where(jnp.abs(col_in - col_out) <= HALF_COLS, 1.0, 0.0).astype(jnp.bfloat16)
+
+    @pl.when(row == 0)
+    def _():
+        top[...] = jnp.zeros_like(top)
+
+    @pl.when(row == rows_n - 1)
+    def _():
+        bot[...] = jnp.zeros_like(bot)
+
     def own_dates():
         for l in range(local):
             wait_rims(me, l)
@@ -166,19 +166,19 @@
     def step(t, carry):
         s_left, s_right = me - 1 - t, me + 1 + t
         for k, l in chunks:
+            @pl.when(s_right < n)
+            def _():
+                to_left(k, s_right, l).wait_recv()
+                pl.when(has_left)(lambda: to_left(k, s_right, l).start())
+                if k == 0:
+                    send_rims(s_right, l)
+
             @pl.when(s_left >= 0)
             def _():
                 to_right(k, s_left, l).wait_recv()
                 pl.when(has_right)(lambda: to_right(k, s_left, l).start())
                 if k == 0:
                     send_rims(s_left, l)
-
-            @pl.when(s_right < n)
-            def _():
-                to_left(k, s_right, l).wait_recv()
-                pl.when(has_left)(lambda: to_left(k, s_right, l).start())
-                if k == 0:
-                    send_rims(s_right, l)
 
             if k == 0 and l == local - 1:
                 pl.when(jnp.logical_and(at_end, t == 0))(own_dates)

time: 19.1 us -> 19.2 us (level)
  no operation moved by 1% of the time
where the time goes in v7:
time: 19.2 us; the launch traced here: 19 us
  Pallas kernels  19 us (99%)
    pallas_call x1, Pallas kernels, body(): pl.pallas_call(functools.partial(gather_kernel, n, rows_n), out_shape=kin...  17.4 us
    pallas_call x1, Pallas kernels, body(): pl.pallas_call(order_kernel, out_shape=kind, in_specs=[pl.BlockSpec(memor...  1.57 us

profile of v7, /device:TPU:1, one launch (start us, length us, event | category | flops | bytes accessed | tf_op | source)
XLA Modules:
  0.0 19.0 jit_solution(11404630297827447479)
XLA Ops:
  0.0 0.0 copy-start
  0.0 17.4 %shard_map.28.coh = f32[2,8,2,16,512]{4,3,2,1,0:T(8,128)S(1)} custom-call(f32[2,2,16,512]{3,2,1,0:T(8,128)} %x_ref.1), custom_call_target="tpu_custom_call" | custom-call | tf_op jit(solution)/shard_map/pallas_call | solution.py:259
  17.4 0.0 copy-done
  17.4 1.6 %shard_map.29 = f32[2,8,2,16,512]{4,3,2,1,0:T(8,128)} custom-call(s32[8]{0:T(128)S(1)} %copy-done, f32[2,8,2,16,512]{4,3,2,1,0:T(8,128)S(1)} %shard_map.28.coh), custom_call_target="tpu_custom_call" | custom-call | tf_op jit(solution)/shard_map/pallas_call | solution.py:285
Async XLA Ops:
  0.0 17.4 %copy-start = (s32[8]{0:T(128)S(1)}, s32[8]{0:T(128)}, u32[]{:S(2)}) copy-start(s32[8]{0:T(128)} %plan_ref.1) | copy-start | bytes 100

commit v8 on v7

--- a/solution.py
+++ b/solution.py
@@ -234,16 +234,10 @@
     def copy(k):
         return pltpu.make_async_copy(coh.at[:, plan_ref[k]], out.at[:, k], sem.at[k])
 
-    def start(k, carry):
+    for k in range(dates):
         copy(k).start()
-        return carry
-
-    def finish(k, carry):
+    for k in range(dates):
         copy(k).wait()
-        return carry
-
-    lax.fori_loop(0, dates, start, 0)
-    lax.fori_loop(0, dates, finish, 0)
 
 
 def body(n, rows_n, stack_data, plan):

time: 19.2 us -> 19.2 us (level)
  no operation moved by 1% of the time
where the time goes in v8:
time: 19.2 us; the launch traced here: 19 us
  Pallas kernels  19 us (99%)
    pallas_call x1, Pallas kernels, body(): pl.pallas_call(functools.partial(gather_kernel, n, rows_n), out_shape=kin...  17.4 us
    pallas_call x1, Pallas kernels, body(): pl.pallas_call(order_kernel, out_shape=kind, in_specs=[pl.BlockSpec(memor...  1.57 us

profile of v8, /device:TPU:1, one launch (start us, length us, event | category | flops | bytes accessed | tf_op | source)
XLA Modules:
  0.0 19.0 jit_solution(8862610704449838456)
XLA Ops:
  0.0 0.0 copy-start
  0.0 17.4 %shard_map.28.coh = f32[2,8,2,16,512]{4,3,2,1,0:T(8,128)S(1)} custom-call(f32[2,2,16,512]{3,2,1,0:T(8,128)} %x_ref.1), custom_call_target="tpu_custom_call" | custom-call | tf_op jit(solution)/shard_map/pallas_call | solution.py:253
  17.4 0.0 copy-done
  17.4 1.6 %shard_map.29 = f32[2,8,2,16,512]{4,3,2,1,0:T(8,128)} custom-call(s32[8]{0:T(128)S(1)} %copy-done, f32[2,8,2,16,512]{4,3,2,1,0:T(8,128)S(1)} %shard_map.28.coh), custom_call_target="tpu_custom_call" | custom-call | tf_op jit(solution)/shard_map/pallas_call | solution.py:279
Async XLA Ops:
  0.0 17.4 %copy-start = (s32[8]{0:T(128)S(1)}, s32[8]{0:T(128)}, u32[]{:S(2)}) copy-start(s32[8]{0:T(128)} %plan_ref.1) | copy-start | bytes 100
